TPU v7x, 32 devices: a whole 2x2x4 slice. The times are simulated.
32 devices in a mesh: grp: 2 (over y), rows: 8 (over z, x), mod: 2 (over core).
Axes of the slice: x: 2, y: 2, z: 4, core: 2. Of those that a mesh axis runs over, the one named last changes fastest.
Arguments:
- queries: bfloat16 [16, 8, 2304], P(('grp', 'rows'), 'mod'), parts along dimension 0, may hold values from -6 to 6
- train_grads: bfloat16 [2048, 8, 2304], P(('grp', 'rows'), 'mod'), parts along dimension 0, may hold values from -6 to 6
- factors: float32 [8, 2, 48, 48], P('mod'), may hold values from -4 to 4, as said below
Outputs:
- scores: float32 [16, 1024], P(('grp', 'mod'), 'rows'), parts along dimension 0
There are 2 independent parts, one for each index of `grp`. A program takes and returns all parts, laid end to end along the dimension named above; an argument that names none is the same for every part. Nothing has to cross between parts.
Inputs may be any that keep to these rules, and one draw needn't show every extreme that they name: `factors`: each factor is a 48 x 48 matrix with a positive diagonal and full rank.
All inputs are finite; a program needn't handle non-finite values.
Results may differ from a plain program's by a relative error of at most 0.0029.
Values may be sent and summed in bfloat16 or wider, within the bound.
No kernel may reach another device: no remote copies, remote signals or barrier semaphores. Data moves between devices by JAX's collectives and lax.ppermute only.
A program may use at most 64 MiB of HBM per device.

v0:
```python
import jax
import jax.numpy as jnp
from jax import lax
from jax.sharding import PartitionSpec as P

MODULES = 8
PROJ = 48
COORDS = 2304


def precondition(grads_in, factors):
    count = grads_in.shape[0]
    local_modules = grads_in.shape[1]
    grads = grads_in.astype(jnp.float32).reshape(count, local_modules, PROJ, PROJ)
    left_side = jnp.einsum("mab,qmbc->qmac", factors[:, 0], grads, precision=lax.Precision.HIGHEST)
    both_sides = jnp.einsum(
        "qmac,mcd->qmad", left_side, factors[:, 1], precision=lax.Precision.HIGHEST
    )
    both_sides = both_sides / jnp.sqrt(jnp.float32(MODULES * COORDS))
    return both_sides.astype(jnp.bfloat16).reshape(count, local_modules, PROJ * PROJ)


def shards(queries, train_grads, factors):
    train_count = train_grads.shape[0]
    train_flat = train_grads.reshape(train_count, -1)
    scaled_own = precondition(queries, factors)
    ready_rows = lax.all_gather(scaled_own, "rows", axis=0, tiled=True)
    flat_rows = ready_rows.reshape(ready_rows.shape[0], -1)
    partial_value = lax.dot_general(
        flat_rows, train_flat, (((1,), (1,)), ((), ())), preferred_element_type=jnp.float32
    )
    return lax.psum_scatter(partial_value, "mod", scatter_dimension=0, tiled=True)


def solution(mesh):
    in_specs = (
        P(("grp", "rows"), "mod", None),
        P(("grp", "rows"), "mod", None),
        P("mod", None, None, None),
    )
    out_specs = P(("grp", "mod"), "rows")
    return jax.shard_map(shards, mesh=mesh, in_specs=in_specs, out_specs=out_specs, check_vma=False)
```

profile of v0, /device:TPU:0, one launch (start us, length us, event | category | flops | bytes accessed | tf_op | source)
XLA Modules:
  0.0 40.9 jit_solution(16463728505834022918)
XLA Ops:
  0.0 0.0 copy-start
  0.0 0.0 copy-start.1
  0.0 1.0 %reshape.18 = bf16[4,48,48]{2,1,0:T(8,128)(2,1)S(1)} reshape(bf16[1,4,2304]{2,1,0:T(4,128)(2,1)} %param.3) | data formatting | bytes 36864 | tf_op jit(solution)/shard_map/reshape
  1.0 1.2 %convolution_bitcast_fusion = f32[4,48,48]{1,2,0:T(8,128)S(1)} fusion(bf16[4,48,48]{2,1,0:T(8,128)(2,1)S(1)} %reshape.18, f32[4,2,48,48]{3,2,1,0:T(8,128)} %param.5), kind=kOutput, calls=%fused_computation.3 | convolution fusion | flops 5308416 | bytes 153600 | tf_op jit(solution)/shard_map/mab,qmbc->qmac/dot_general | solution.py:15
  2.1 1.2 %fusion.3 = bf16[1,4,48,48]{3,2,1,0:T(8,128)(2,1)S(1)} fusion(f32[4,48,48]{1,2,0:T(8,128)S(1)} %convolution_bitcast_fusion, f32[4,2,48,48]{3,2,1,0:T(8,128)} %param.5), kind=kOutput, calls=%fused_computation.5 | convolution fusion | flops 5326848 | bytes 153600 | tf_op jit(solution)/shard_map/qmac,mcd->qmad/dot_general | solution.py:16
  3.4 0.1 reshape.20
  3.5 32.4 %all_gather.3 = bf16[8,4,2304]{2,1,0:T(4,128)(2,1)S(1)} all-gather(bf16[1,4,2304]{2,1,0:T(4,128)(2,1)S(1)} %reshape.20), channel_id=1, replica_groups=mesh['grp'=2,'rows'=8,'mod'=2] {'rows'}, dimensions={0}, use_global_device_ids=true | all-gather | bytes 165888 | tf_op jit(solution)/shard_map/all_gather | solution.py:27
  35.9 0.0 copy-done
  35.9 0.7 %fusion.4 = f32[8,128]{1,0:T(8,128)S(1)} fusion(bf16[128,4,2304]{2,1,0:T(4,128)(2,1)S(1)} %copy-done, bf16[8,4,2304]{2,1,0:T(4,128)(2,1)S(1)} %all_gather.3), kind=kOutput, calls=%fused_computation.6 | convolution fusion | flops 18874368 | bytes 2510848 | tf_op jit(solution)/shard_map/dot_general | solution.py:29
  36.6 2.5 %all-reduce = f32[8,128]{1,0:T(8,128)S(1)} all-reduce(f32[8,128]{1,0:T(8,128)S(1)} %fusion.4), channel_id=2, replica_groups=mesh['grp'=2,'rows'=8,'mod'=2] {'mod'}, use_global_device_ids=true, to_apply=%region_0.0.clone | all-reduce | flops 1024 | bytes 8192
  39.1 0.0 copy-done.1
  39.1 0.6 %dynamic-slice = u32[1]{0:T(128)} dynamic-slice(u32[32]{0:T(128)S(1)} %copy-done.1, u32[]{:T(128)S(6)} %add.3), dynamic_slice_sizes={1} | dynamic-slice | bytes 12
  40.3 0.6 %constant_dynamic-slice_fusion = f32[4,128]{1,0:T(4,128)} fusion(f32[8,128]{1,0:T(8,128)S(1)} %all-reduce, u32[]{:T(128)S(6)} %multiply.5), kind=kLoop, calls=%fused_computation.12 | loop fusion | bytes 4100
Async XLA Ops:
  0.0 35.9 %copy-start = (bf16[128,4,2304]{2,1,0:T(4,128)(2,1)S(1)}, bf16[128,4,2304]{2,1,0:T(4,128)(2,1)}, u32[]{:S(2)}) copy-start(bf16[128,4,2304]{2,1,0:T(4,128)(2,1)} %param.4) | copy-start | bytes 7077892
  0.0 39.1 %copy-start.1 = (u32[32]{0:T(128)S(1)}, u32[32]{0:T(128)}, u32[]{:S(2)}) copy-start(u32[32]{0:T(128)} %constant.6) | copy-start | bytes 388
where the time goes:
time: 41.1 us; the launch traced here: 40.9 us
  blocking collectives  34.8 us (85%)
  matrix products  3.1 us (8%)
  local copies, waits for them, and re-layouts  2.27 us (6%)
  between operations  0.68 us (2%)
    all_gather x1, blocking collectives, shards(): ready_rows = lax.all_gather(scaled_own, 'rows', axis=0, tiled=True)  32.4 us
    unnamed x1, blocking collectives  2.46 us
    dot_general x1, matrix products, precondition(): jnp.einsum('qmac,mcd->qmad', left_side, factors[:, 1], precision=lax.Prec...  1.24 us
    unnamed x6, local copies, waits for them, and re-layouts  1.18 us
    dot_general x1, matrix products, precondition(): jnp.einsum('mab,qmbc->qmac', factors[:, 0], grads, precision=lax.Precisio...  1.15 us
    reshape x1, local copies, waits for them, and re-layouts  0.98 us

commit v1 on v0

--- a/solution.py
+++ b/solution.py
@@ -6,6 +6,23 @@
 MODULES = 8
 PROJ = 48
 COORDS = 2304
+
+
+def joined_along(pieces, dim):
+    pieces = jnp.moveaxis(pieces, 0, dim)
+    lengths = pieces.shape
+    return pieces.reshape(*lengths[:dim], lengths[dim] * lengths[dim + 1], *lengths[dim + 2 :])
+
+
+def ring_gather(shard, axis, dim):
+    peers = lax.axis_size(axis)
+    upward = [(i, (i + 1) % peers) for i in range(peers)]
+    blocks = [shard]
+    while len(blocks) < peers:
+        blocks.append(lax.ppermute(blocks[-1], axis, upward))
+    index = lax.axis_index(axis)
+    blocks = jnp.stack(blocks)[(index - jnp.arange(peers)) % peers]
+    return joined_along(blocks, dim)
 
 
 def precondition(grads_in, factors):
@@ -24,7 +41,7 @@
     train_count = train_grads.shape[0]
     train_flat = train_grads.reshape(train_count, -1)
     scaled_own = precondition(queries, factors)
-    ready_rows = lax.all_gather(scaled_own, "rows", axis=0, tiled=True)
+    ready_rows = ring_gather(scaled_own, "rows", 0)
     flat_rows = ready_rows.reshape(ready_rows.shape[0], -1)
     partial_value = lax.dot_general(
         flat_rows, train_flat, (((1,), (1,)), ((), ())), preferred_element_type=jnp.float32

time: 41.1 us -> 54.7 us (1.33)
  waiting for transfers between devices: 0 us -> 39.8 us
  blocking collectives: 34.8 us -> 2.47 us
  starting transfers between devices: 0 us -> 3.29 us
  local copies, waits for them, and re-layouts: 2.27 us -> 5.01 us
    ppermute x0 -> x7, waiting for transfers between devices: none -> 39.8 us  [ring_gather(): blocks.append(lax.ppermute(blocks[-1], axis, upward))]
    all_gather x1 -> x0, blocking collectives: 32.4 us -> none  [shards(): ready_rows = lax.all_gather(scaled_own, 'rows', axis=0, tiled=True)]
    ppermute x0 -> x7, starting transfers between devices: none -> 3.29 us  [ring_gather(): blocks.append(lax.ppermute(blocks[-1], axis, upward))]
    unnamed x6 -> x13, local copies, waits for them, and re-layouts: 1.18 us -> 3.27 us
    gather x0 -> x1, local copies, waits for them, and re-layouts: none -> 0.67 us  [ring_gather(): blocks = jnp.stack(blocks)[(index - jnp.arange(peers)) % peers]]
  transfers between devices with their start and end apart: 0 -> 7, of which waited for: 0 -> 7; matrix products, arithmetic and copies ran while one was open for 0% -> 5% of each run, Pallas kernels for 0% -> 0%
where the time goes in v1:
time: 54.7 us; the launch traced here: 54.4 us
  waiting for transfers between devices  39.8 us (73%)
  local copies, waits for them, and re-layouts  5.01 us (9%)
  starting transfers between devices  3.29 us (6%)
  matrix products  3.09 us (6%)
  blocking collectives  2.47 us (5%)
  between operations  0.78 us (1%)
    ppermute x7, waiting for transfers between devices, ring_gather(): blocks.append(lax.ppermute(blocks[-1], axis, upward))  39.8 us
    ppermute x7, starting transfers between devices, ring_gather(): blocks.append(lax.ppermute(blocks[-1], axis, upward))  3.29 us
    unnamed x13, local copies, waits for them, and re-layouts  3.27 us
    unnamed x1, blocking collectives  2.47 us
    dot_general x1, matrix products, precondition(): jnp.einsum('qmac,mcd->qmad', left_side, factors[:, 1], precision=lax.Prec...  1.24 us
    dot_general x1, matrix products, precondition(): jnp.einsum('mab,qmbc->qmac', factors[:, 0], grads, precision=lax.Precisio...  1.15 us
  transfers between devices with their start and end apart: 7, of which 7 were waited for; matrix products, arithmetic and copies ran while one was open for 5% of the time, Pallas kernels for 0%

profile of v1, /device:TPU:0, one launch (start us, length us, event | category | flops | bytes accessed | tf_op | source)
XLA Modules:
  0.0 54.4 jit_solution(12559932915170992699)
XLA Ops:
  0.0 0.8 %reshape.68 = bf16[4,48,48]{2,1,0:T(8,128)(2,1)S(1)} reshape(bf16[1,4,2304]{2,1,0:T(4,128)(2,1)} %param.3) | data formatting | bytes 36864 | tf_op jit(solution)/shard_map/reshape
  0.8 1.2 %convolution_bitcast_fusion = f32[4,48,48]{1,2,0:T(8,128)S(1)} fusion(bf16[4,48,48]{2,1,0:T(8,128)(2,1)S(1)} %reshape.68, f32[4,2,48,48]{3,2,1,0:T(8,128)} %param.5), kind=kOutput, calls=%fused_computation.2 | convolution fusion | flops 5308416 | bytes 153600 | tf_op jit(solution)/shard_map/mab,qmbc->qmac/dot_general | solution.py:32
  2.0 1.2 %fusion.1 = bf16[1,4,48,48]{3,2,1,0:T(8,128)(2,1)S(1)} fusion(f32[4,48,48]{1,2,0:T(8,128)S(1)} %convolution_bitcast_fusion, f32[4,2,48,48]{3,2,1,0:T(8,128)} %param.5), kind=kOutput, calls=%fused_computation.4 | convolution fusion | flops 5326848 | bytes 153600 | tf_op jit(solution)/shard_map/qmac,mcd->qmad/dot_general | solution.py:33
  3.2 0.1 reshape.70
  3.4 3.0 %collective-permute-start = (bf16[1,4,2304]{2,1,0:T(4,128)(2,1)S(1)}, bf16[1,4,2304]{2,1,0:T(4,128)(2,1)S(1)}, u32[]{:S(2)}, u32[]{:S(2)}) collective-permute-start(bf16[1,4,2304]{2,1,0:T(4,128)(2,1)S(1)} %reshape.70), channel_id=1, source_target_pairs={{0,2},{2,4},{4,6},{6,8},{8,10},{10,12},{12,14},{14,0},{1,3},{3,5},... | collective-permute-start | bytes 55304 | tf_op jit(solution)/shard_map/ppermute | solution.py:22
  6.4 0.1 stack_reshape.3
  6.6 0.0 copy-start
  6.6 2.0 %copy.17 = bf16[16,8,4,2304]{3,1,2,0:T(8,128)(2,1)S(1)} copy(bf16[16,8,4,2304]{3,2,1,0:T(4,128)(2,1)} %bitcast.53) | data formatting | bytes 4718592
  8.6 0.0 copy-done
  8.6 0.6 %dynamic-slice = u32[1]{0:T(128)} dynamic-slice(u32[32]{0:T(128)S(1)} %copy-done, u32[]{:T(128)S(6)} %add.28), dynamic_slice_sizes={1} | dynamic-slice | bytes 12
  9.8 1.4 %collective-permute-done = bf16[1,4,2304]{2,1,0:T(4,128)(2,1)S(1)} collective-permute-done((bf16[1,4,2304]{2,1,0:T(4,128)(2,1)S(1)}, bf16[1,4,2304]{2,1,0:T(4,128)(2,1)S(1)}, u32[]{:S(2)}, u32[]{:S(2)}) %collective-permute-start) | collective-permute-done | bytes 18464 | tf_op jit(solution)/shard_map/ppermute | solution.py:22
  11.2 0.3 collective-permute-start.1
  11.4 6.2 %collective-permute-done.1 = bf16[1,4,2304]{2,1,0:T(4,128)(2,1)S(1)} collective-permute-done((bf16[1,4,2304]{2,1,0:T(4,128)(2,1)S(1)}, bf16[1,4,2304]{2,1,0:T(4,128)(2,1)S(1)}, u32[]{:S(2)}, u32[]{:S(2)}) %collective-permute-start.1) | collective-permute-done | bytes 18464 | tf_op jit(solution)/shard_map/ppermute | solution.py:22
  17.6 0.0 collective-permute-start.2
  17.6 6.4 %collective-permute-done.2 = bf16[1,4,2304]{2,1,0:T(4,128)(2,1)S(1)} collective-permute-done((bf16[1,4,2304]{2,1,0:T(4,128)(2,1)S(1)}, bf16[1,4,2304]{2,1,0:T(4,128)(2,1)S(1)}, u32[]{:S(2)}, u32[]{:S(2)}) %collective-permute-start.2) | collective-permute-done | bytes 18464 | tf_op jit(solution)/shard_map/ppermute | solution.py:22
  24.1 0.0 collective-permute-start.3
  24.1 6.4 %collective-permute-done.3 = bf16[1,4,2304]{2,1,0:T(4,128)(2,1)S(1)} collective-permute-done((bf16[1,4,2304]{2,1,0:T(4,128)(2,1)S(1)}, bf16[1,4,2304]{2,1,0:T(4,128)(2,1)S(1)}, u32[]{:S(2)}, u32[]{:S(2)}) %collective-permute-start.3) | collective-permute-done | bytes 18464 | tf_op jit(solution)/shard_map/ppermute | solution.py:22
  30.5 0.0 collective-permute-start.4
  30.6 6.5 %collective-permute-done.4 = bf16[1,4,2304]{2,1,0:T(4,128)(2,1)S(1)} collective-permute-done((bf16[1,4,2304]{2,1,0:T(4,128)(2,1)S(1)}, bf16[1,4,2304]{2,1,0:T(4,128)(2,1)S(1)}, u32[]{:S(2)}, u32[]{:S(2)}) %collective-permute-start.4) | collective-permute-done | bytes 18464 | tf_op jit(solution)/shard_map/ppermute | solution.py:22
  37.0 0.0 collective-permute-start.5
  37.1 6.4 %collective-permute-done.5 = bf16[1,4,2304]{2,1,0:T(4,128)(2,1)S(1)} collective-permute-done((bf16[1,4,2304]{2,1,0:T(4,128)(2,1)S(1)}, bf16[1,4,2304]{2,1,0:T(4,128)(2,1)S(1)}, u32[]{:S(2)}, u32[]{:S(2)}) %collective-permute-start.5) | collective-permute-done | bytes 18464 | tf_op jit(solution)/shard_map/ppermute | solution.py:22
  43.5 0.0 collective-permute-start.6
  43.5 6.4 %collective-permute-done.6 = bf16[1,4,2304]{2,1,0:T(4,128)(2,1)S(1)} collective-permute-done((bf16[1,4,2304]{2,1,0:T(4,128)(2,1)S(1)}, bf16[1,4,2304]{2,1,0:T(4,128)(2,1)S(1)}, u32[]{:S(2)}, u32[]{:S(2)}) %collective-permute-start.6) | collective-permute-done | bytes 18464 | tf_op jit(solution)/shard_map/ppermute | solution.py:22
  50.0 0.7 %gather_fusion = bf16[8,4,2304]{2,1,0:T(4,128)(2,1)S(1)} fusion(bf16[8,4,2304]{2,1,0:T(4,128)(2,1)S(1)} %bitcast.56, s32[1024]{0:T(1024)S(1)} %pad_clamp_fusion), kind=kCustom, calls=%fused_computation | custom fusion | bytes 294944 | tf_op jit(solution)/shard_map/gather | solution.py:24
  50.7 0.7 %fusion.8 = f32[8,128]{1,0:T(8,128)S(1)} fusion(bf16[8,9216]{1,0:T(8,128)(2,1)S(1)} %bitcast.54, bf16[128,9216]{1,0:T(8,128)(2,1)S(1)} %bitcast.52), kind=kOutput, calls=%fused_computation.25 | convolution fusion | flops 18874368 | bytes 2510848 | tf_op jit(solution)/shard_map/dot_general | solution.py:46
  51.4 2.5 %all-reduce = f32[8,128]{1,0:T(8,128)S(1)} all-reduce(f32[8,128]{1,0:T(8,128)S(1)} %fusion.8), channel_id=2, replica_groups=mesh['grp'=2,'rows'=8,'mod'=2] {'mod'}, use_global_device_ids=true, to_apply=%region_0.1.clone | all-reduce | flops 1024 | bytes 8192
  53.9 0.6 %constant_dynamic-slice_fusion = f32[4,128]{1,0:T(4,128)} fusion(f32[8,128]{1,0:T(8,128)S(1)} %all-reduce, u32[]{:T(128)S(6)} %multiply.5), kind=kLoop, calls=%fused_computation.24 | loop fusion | bytes 4100
  (11 shorter events, 0.2 us)
Async XLA Ops:
  3.4 7.8 %collective-permute-start = (bf16[1,4,2304]{2,1,0:T(4,128)(2,1)S(1)}, bf16[1,4,2304]{2,1,0:T(4,128)(2,1)S(1)}, u32[]{:S(2)}, u32[]{:S(2)}) collective-permute-start(bf16[1,4,2304]{2,1,0:T(4,128)(2,1)S(1)} %reshape.70), channel_id=1, source_target_pairs={{0,2},{2,4},{4,6},{6,8},{8,10},{10,12},{12,14},{14,0},{1,3},{3,5},... | collective-permute-start | bytes 55304 | tf_op jit(solution)/shard_map/ppermute | solution.py:22
  6.6 2.0 %copy-start = (u32[32]{0:T(128)S(1)}, u32[32]{0:T(128)}, u32[]{:S(2)}) copy-start(u32[32]{0:T(128)} %constant.29) | copy-start | bytes 388
  11.2 6.5 %collective-permute-start.1 = (bf16[1,4,2304]{2,1,0:T(4,128)(2,1)S(1)}, bf16[1,4,2304]{2,1,0:T(4,128)(2,1)S(1)}, u32[]{:S(2)}, u32[]{:S(2)}) collective-permute-start(bf16[1,4,2304]{2,1,0:T(4,128)(2,1)S(1)} %collective-permute-done), channel_id=1, source_target_pairs={{0,2},{2,4},{4,6},{6,8},{8,10},{10,12},{12,14},{14,0},{1,3},{3,5},... | collective-permute-start | bytes 55304 | tf_op jit(solution)/shard_map/ppermute | solution.py:22
  17.6 6.5 %collective-permute-start.2 = (bf16[1,4,2304]{2,1,0:T(4,128)(2,1)S(1)}, bf16[1,4,2304]{2,1,0:T(4,128)(2,1)S(1)}, u32[]{:S(2)}, u32[]{:S(2)}) collective-permute-start(bf16[1,4,2304]{2,1,0:T(4,128)(2,1)S(1)} %collective-permute-done.1), channel_id=1, source_target_pairs={{0,2},{2,4},{4,6},{6,8},{8,10},{10,12},{12,14},{14,0},{1,3},{3,5},... | collective-permute-start | bytes 55304 | tf_op jit(solution)/shard_map/ppermute | solution.py:22
  24.1 6.5 %collective-permute-start.3 = (bf16[1,4,2304]{2,1,0:T(4,128)(2,1)S(1)}, bf16[1,4,2304]{2,1,0:T(4,128)(2,1)S(1)}, u32[]{:S(2)}, u32[]{:S(2)}) collective-permute-start(bf16[1,4,2304]{2,1,0:T(4,128)(2,1)S(1)} %collective-permute-done.2), channel_id=1, source_target_pairs={{0,2},{2,4},{4,6},{6,8},{8,10},{10,12},{12,14},{14,0},{1,3},{3,5},... | collective-permute-start | bytes 55304 | tf_op jit(solution)/shard_map/ppermute | solution.py:22
  30.5 6.5 %collective-permute-start.4 = (bf16[1,4,2304]{2,1,0:T(4,128)(2,1)S(1)}, bf16[1,4,2304]{2,1,0:T(4,128)(2,1)S(1)}, u32[]{:S(2)}, u32[]{:S(2)}) collective-permute-start(bf16[1,4,2304]{2,1,0:T(4,128)(2,1)S(1)} %collective-permute-done.3), channel_id=1, source_target_pairs={{0,2},{2,4},{4,6},{6,8},{8,10},{10,12},{12,14},{14,0},{1,3},{3,5},... | collective-permute-start | bytes 55304 | tf_op jit(solution)/shard_map/ppermute | solution.py:22
  37.0 6.5 %collective-permute-start.5 = (bf16[1,4,2304]{2,1,0:T(4,128)(2,1)S(1)}, bf16[1,4,2304]{2,1,0:T(4,128)(2,1)S(1)}, u32[]{:S(2)}, u32[]{:S(2)}) collective-permute-start(bf16[1,4,2304]{2,1,0:T(4,128)(2,1)S(1)} %collective-permute-done.4), channel_id=1, source_target_pairs={{0,2},{2,4},{4,6},{6,8},{8,10},{10,12},{12,14},{14,0},{1,3},{3,5},... | collective-permute-start | bytes 55304 | tf_op jit(solution)/shard_map/ppermute | solution.py:22
  43.5 6.5 %collective-permute-start.6 = (bf16[1,4,2304]{2,1,0:T(4,128)(2,1)S(1)}, bf16[1,4,2304]{2,1,0:T(4,128)(2,1)S(1)}, u32[]{:S(2)}, u32[]{:S(2)}) collective-permute-start(bf16[1,4,2304]{2,1,0:T(4,128)(2,1)S(1)} %collective-permute-done.5), channel_id=1, source_target_pairs={{0,2},{2,4},{4,6},{6,8},{8,10},{10,12},{12,14},{14,0},{1,3},{3,5},... | collective-permute-start | bytes 55304 | tf_op jit(solution)/shard_map/ppermute | solution.py:22
